TPU v7x, 32 devices: a whole 2x2x4 slice. The times are simulated.
32 devices in a mesh: job: 2 (over x), tm: 2 (over core), rows: 8 (over z, y).
Axes of the slice: x: 2, y: 2, z: 4, core: 2. Of those that a mesh axis runs over, the one named last changes fastest.
Arguments:
- prior: bfloat16 [2, 524288, 64], P('tm', ('job', 'rows')), parts along dimension 1, may hold values from -80 to 80
- snapshots: bfloat16 [2, 524288, 256], P('tm', ('job', 'rows')), parts along dimension 1, may hold values from -60 to 60
Outputs:
- merged: bfloat16 [524288, 64], P(('job', 'rows'), 'tm'), parts along dimension 0
There are 2 independent parts, one for each index of `job`. A program takes and returns all parts, laid end to end along the dimension named above; each array names one. Nothing has to cross between parts.
All inputs are finite; a program needn't handle non-finite values.
Results may differ from a plain program's by a relative error of at most 0.011.
Values may be sent and summed in bfloat16 or wider, within the bound.
A program may use at most 128 MiB of HBM per device.

v0:
```python
import jax
import jax.numpy as jnp
from jax import lax
from jax.sharding import PartitionSpec as P

STEPS = 4
ITERS = 2


def partner(block, axis, bit):
    count = lax.axis_size(axis)
    route = []
    for low in range(count):
        high = low | 1 << bit
        if high != low and high < count:
            route += [(low, high), (high, low)]
    return lax.ppermute(block, axis, route)


def basis_of(gram, keep):
    order = gram.shape[0]
    basis = jnp.eye(order, keep, dtype=jnp.float32)
    for turn in range(ITERS):
        image = jnp.dot(gram, basis, precision=lax.Precision.HIGHEST)
        inner = jnp.dot(image.T, image, precision=lax.Precision.HIGHEST)
        lower = jnp.linalg.cholesky(inner)
        basis = jax.scipy.linalg.solve_triangular(lower, image.T, lower=True).T
    return basis


def project(joined, basis):
    return jnp.dot(
        joined, basis, precision=lax.Precision.HIGHEST, preferred_element_type=jnp.float32
    )


def inner_rows(left, right):
    return jnp.dot(
        left.T, right, precision=lax.Precision.HIGHEST, preferred_element_type=jnp.float32
    )


def shards(prior, snapshots):
    start_modes = prior[0]
    frames = snapshots[0]
    keep = start_modes.shape[1]
    fresh_cols = frames.shape[1] // STEPS
    whole = jnp.concatenate([start_modes, frames], axis=1)
    total = lax.psum(jnp.dot(whole.T, whole, preferred_element_type=jnp.float32), "rows")
    width = whole.shape[1]
    weights = jnp.eye(width, keep, dtype=jnp.float32)
    for step in range(STEPS):
        picker = jnp.eye(width, fresh_cols, k=-(keep + step * fresh_cols), dtype=jnp.float32)
        coeffs = jnp.concatenate([weights, picker], axis=1)
        applied = jnp.dot(total, coeffs, precision=lax.Precision.HIGHEST)
        gram = jnp.dot(coeffs.T, applied, precision=lax.Precision.HIGHEST)
        weights = jnp.dot(coeffs, basis_of(gram, keep), precision=lax.Precision.HIGHEST)
    modes = project(whole, weights)
    index = lax.axis_index("tm")
    half_keep = keep // 2
    other = partner(modes.astype(jnp.bfloat16), "tm", 0).astype(modes.dtype)
    first = jnp.where(index == 0, modes, other)
    second = jnp.where(index == 0, other, modes)
    joined = jnp.concatenate([first, second], axis=1)
    gram = lax.psum(inner_rows(joined, joined).astype(jnp.bfloat16), "rows").astype(jnp.float32)
    full_merge = project(joined, basis_of(gram, keep)).astype(jnp.bfloat16)
    merged = lax.dynamic_slice_in_dim(full_merge, index * half_keep, half_keep, 1)
    return merged


def solution(mesh):
    in_specs = (P("tm", ("job", "rows"), None), P("tm", ("job", "rows"), None))
    out_specs = P(("job", "rows"), "tm")
    return jax.shard_map(shards, mesh=mesh, in_specs=in_specs, out_specs=out_specs, check_vma=False)
```

profile of v0, /device:TPU:0, one launch (start us, length us, event | category | flops | bytes accessed | tf_op | source)
XLA Modules:
  0.0 384.4 jit_solution(9080420248376913407)
XLA Ops:
  6.5 8.5 %copy.3 = bf16[1,32768,64]{2,1,0:T(8,128)(2,1)} copy(bf16[1,32768,64]{1,2,0:T(8,128)(2,1)} %param.5) | data formatting | bytes 8388608 | tf_op args[0]
  15.0 31.2 %fusion.1 = f32[320,320]{1,0:T(8,128)} fusion(bf16[32768,256]{1,0:T(8,128)(2,1)} %bitcast.173, bf16[32768,64]{1,0:T(8,128)(2,1)} %bitcast.171), kind=kOutput, calls=%fused_computation.3 | convolution fusion | flops 6752829440 | bytes 21381120 | tf_op jit(solution)/shard_map/dot_general | solution.py:49
  46.4 75.3 %all-reduce.2.cloned.1.call-done = f32[320,320]{1,0:T(8,128)} async-done(((f32[320,320]{1,0:T(8,128)}), f32[320,320]{1,0:T(8,128)}) %all-reduce.2.cloned.1.call-update) | async-done | bytes 409616 | tf_op jit(solution)/shard_map/psum | solution.py:49
  124.1 5.8 %cholesky.164 = f32[64,64]{1,0:T(8,128)S(1)} custom-call(f32[64,64]{1,0:T(8,128)S(1)} %fusion.71), custom_call_target="Cholesky" | custom-call | tf_op jit(solution)/shard_map/jit(cholesky)/cholesky | solution.py:26
  137.0 5.8 %cholesky.175 = f32[64,64]{1,0:T(8,128)S(1)} custom-call(f32[64,64]{1,0:T(8,128)S(1)} %fusion.67), custom_call_target="Cholesky" | custom-call | tf_op jit(solution)/shard_map/jit(cholesky)/cholesky | solution.py:26
  144.2 4.9 %custom-call.15 = f32[1,64,64]{1,2,0:T(8,128)S(1)} custom-call(f32[1,64,64]{2,1,0:T(8,128)S(1)} %fusion.23), custom_call_target="InvertDiagBlocksLowerTriangular" | custom-call | tf_op jit(solution)/shard_map/jit(_solve_triangular)/triangular_solve | solution.py:27
  152.1 5.8 %cholesky.186 = f32[64,64]{1,0:T(8,128)S(1)} custom-call(f32[64,64]{1,0:T(8,128)S(1)} %fusion.63), custom_call_target="Cholesky" | custom-call | tf_op jit(solution)/shard_map/jit(cholesky)/cholesky | solution.py:26
  159.3 4.9 %custom-call.16 = f32[1,64,64]{1,2,0:T(8,128)S(1)} custom-call(f32[1,64,64]{2,1,0:T(8,128)S(1)} %fusion.24), custom_call_target="InvertDiagBlocksLowerTriangular" | custom-call | tf_op jit(solution)/shard_map/jit(_solve_triangular)/triangular_solve | solution.py:27
  165.0 5.8 %cholesky.197 = f32[64,64]{1,0:T(8,128)S(1)} custom-call(f32[64,64]{1,0:T(8,128)S(1)} %fusion.59), custom_call_target="Cholesky" | custom-call | tf_op jit(solution)/shard_map/jit(cholesky)/cholesky | solution.py:26
  172.2 4.9 %custom-call.17 = f32[1,64,64]{1,2,0:T(8,128)S(1)} custom-call(f32[1,64,64]{2,1,0:T(8,128)S(1)} %fusion.25), custom_call_target="InvertDiagBlocksLowerTriangular" | custom-call | tf_op jit(solution)/shard_map/jit(_solve_triangular)/triangular_solve | solution.py:27
  180.1 6.0 %cholesky.208 = f32[64,64]{1,0:T(8,128)S(1)} custom-call(f32[64,64]{1,0:T(8,128)S(1)} %fusion.55), custom_call_target="Cholesky" | custom-call | tf_op jit(solution)/shard_map/jit(cholesky)/cholesky | solution.py:26
  187.4 4.9 %custom-call.18 = f32[1,64,64]{1,2,0:T(8,128)S(1)} custom-call(f32[1,64,64]{2,1,0:T(8,128)S(1)} %fusion.26), custom_call_target="InvertDiagBlocksLowerTriangular" | custom-call | tf_op jit(solution)/shard_map/jit(_solve_triangular)/triangular_solve | solution.py:27
  193.1 5.8 %cholesky.219 = f32[64,64]{1,0:T(8,128)S(1)} custom-call(f32[64,64]{1,0:T(8,128)S(1)} %fusion.51), custom_call_target="Cholesky" | custom-call | tf_op jit(solution)/shard_map/jit(cholesky)/cholesky | solution.py:26
  200.3 4.9 %custom-call.19 = f32[1,64,64]{1,2,0:T(8,128)S(1)} custom-call(f32[1,64,64]{2,1,0:T(8,128)S(1)} %fusion.27), custom_call_target="InvertDiagBlocksLowerTriangular" | custom-call | tf_op jit(solution)/shard_map/jit(_solve_triangular)/triangular_solve | solution.py:27
  208.2 5.8 %cholesky.230 = f32[64,64]{1,0:T(8,128)S(1)} custom-call(f32[64,64]{1,0:T(8,128)S(1)} %fusion.47), custom_call_target="Cholesky" | custom-call | tf_op jit(solution)/shard_map/jit(cholesky)/cholesky | solution.py:26
  221.0 5.8 %cholesky.241 = f32[64,64]{1,0:T(8,128)S(1)} custom-call(f32[64,64]{1,0:T(8,128)S(1)} %fusion.43), custom_call_target="Cholesky" | custom-call | tf_op jit(solution)/shard_map/jit(cholesky)/cholesky | solution.py:26
  233.9 28.9 %fusion.90 = (bf16[32768,64]{0,1:T(8,128)(2,1)}, f32[32768,64]{0,1:T(8,128)}) fusion(f32[320,64]{1,0:T(8,128)S(1)} %fusion.5, bf16[32768,256]{1,0:T(8,128)(2,1)} %bitcast.174, bf16[32768,64]{1,0:T(8,128)(2,1)} %bitcast.172), kind=kOutput, calls=%fused_computation.150 | convolution fusion | flops 8097103872 | bytes 33636352 | tf_op jit(solution)/shard_map/dot_general | solution.py:32
  262.7 7.5 %collective-permute-done = bf16[32768,64]{0,1:T(8,128)(2,1)} collective-permute-done((bf16[32768,64]{0,1:T(8,128)(2,1)}, bf16[32768,64]{0,1:T(8,128)(2,1)}, u32[]{:S(2)}, u32[]{:S(2)}) %collective-permute-start) | collective-permute-done | bytes 4194336 | tf_op jit(solution)/shard_map/ppermute | solution.py:17
  270.2 12.1 %convert_select_fusion.1 = (f32[32768,64]{0,1:T(8,128)}, f32[32768,64]{0,1:T(8,128)}) fusion(f32[32768,64]{0,1:T(8,128)} %get-tuple-element.10, bf16[32768,64]{0,1:T(8,128)(2,1)} %collective-permute-done, pred[]{:T(512)S(6)} %eq.34), kind=kLoop, calls=%fused_computation.7 | loop fusion | flops 6291456 | bytes 29360128 | tf_op jit(solution)/shard_map/jit(_where)/select_n | solution.py:62
  282.3 18.3 %fusion.4 = bf16[128,128]{1,0:T(8,128)(2,1)S(1)} fusion(f32[32768,64]{0,1:T(8,128)} %get-tuple-element.8, f32[32768,64]{0,1:T(8,128)} %get-tuple-element.6), kind=kOutput, calls=%fused_computation.9 | convolution fusion | flops 6446661632 | bytes 16809984 | tf_op jit(solution)/shard_map/dot_general | solution.py:38
  300.7 35.5 %psum.15 = bf16[128,128]{1,0:T(8,128)(2,1)S(1)} all-reduce(bf16[128,128]{1,0:T(8,128)(2,1)S(1)} %fusion.4), channel_id=1, replica_groups=mesh['job'=2,'tm'=2,'rows'=8] {'rows'}, use_global_device_ids=true, to_apply=%region_3.6 | all-reduce | flops 16384 | bytes 65536 | tf_op jit(solution)/shard_map/psum | solution.py:65
  336.6 5.8 %cholesky.252 = f32[64,64]{1,0:T(8,128)S(1)} custom-call(f32[64,64]{1,0:T(8,128)S(1)} %fusion.39), custom_call_target="Cholesky" | custom-call | tf_op jit(solution)/shard_map/jit(cholesky)/cholesky | solution.py:26
  349.5 5.8 %cholesky.263 = f32[64,64]{1,0:T(8,128)S(1)} custom-call(f32[64,64]{1,0:T(8,128)S(1)} %fusion.35), custom_call_target="Cholesky" | custom-call | tf_op jit(solution)/shard_map/jit(cholesky)/cholesky | solution.py:26
  361.8 13.8 %fusion.2 = bf16[32768,64]{0,1:T(8,128)(2,1)S(1)} fusion(f32[64,128]{1,0:T(8,128)S(1)} %fusion.32, f32[32768,64]{0,1:T(8,128)} %get-tuple-element.8, f32[32768,64]{0,1:T(8,128)} %get-tuple-element.6), kind=kOutput, calls=%fused_computation.4 | convolution fusion | flops 3225419776 | bytes 21004288 | tf_op jit(solution)/shard_map/dot_general | solution.py:32
  (109 shorter events, 55.8 us)
Async XLA Ops:
  6.5 115.2 %all-reduce.2.cloned.1.call-start = ((), (), s32[]{:S(2)}) async-start(), calls=%async_computation | async-start | bytes 983040 | tf_op jit(solution)/shard_map/psum | solution.py:49
  262.7 7.5 %collective-permute-start = (bf16[32768,64]{0,1:T(8,128)(2,1)}, bf16[32768,64]{0,1:T(8,128)(2,1)}, u32[]{:S(2)}, u32[]{:S(2)}) collective-permute-start(bf16[32768,64]{0,1:T(8,128)(2,1)} %get-tuple-element.9), channel_id=1, source_target_pairs={{0,8},{8,0},{1,9},{9,1},{2,10},{10,2},{3,11},{11,3},{4,12},{12,4},... | collective-permute-start | bytes 12582920 | tf_op jit(solution)/shard_map/ppermute | solution.py:17
Sparse Core Ops, SparseCore 0:
  46.3 75.3 all-reduce.1
where the time goes:
time: 389 us; the launch traced here: 384 us
  other arithmetic  133 us (34%)
  matrix products  108 us (28%)
  waiting for transfers between devices  82.8 us (21%)
  blocking collectives  35.5 us (9%)
  between operations  14.4 us (4%)
  local copies, waits for them, and re-layouts  10.7 us (3%)
    psum x1, waiting for transfers between devices, shards(): lax.psum(jnp.dot(whole.T, whole, preferred_element_type=jnp.float32), 'ro...  75.3 us
    another operation x30, other arithmetic, basis_of(): lower = jnp.linalg.cholesky(inner)  65.3 us
    another operation x20, other arithmetic, basis_of(): basis = jax.scipy.linalg.solve_triangular(lower, image.T, lower=True).T  55.5 us
    dot_general x2, matrix products, project(): jnp.dot(joined, basis, precision=lax.Precision.HIGHEST, preferred_element...  42.7 us
    psum x1, blocking collectives, shards(): lax.psum(inner_rows(joined, joined).astype(jnp.bfloat16), 'rows')  35.5 us
    dot_general x1, matrix products, shards(): jnp.dot(whole.T, whole, preferred_element_type=jnp.float32)  31.2 us
    dot_general x1, matrix products, inner_rows(): jnp.dot(left.T, right, precision=lax.Precision.HIGHEST, preferred_element...  18.3 us
    select_n x1, other arithmetic, shards(): first = jnp.where(index == 0, modes, other)  12.1 us
  transfers between devices with their start and end apart: 2, of which 2 were waited for; matrix products, arithmetic and copies ran while one was open for 0% of the time, Pallas kernels for 0%

commit v1 on v0

v1 whole, which is shorter than its diff:
```python
import functools

import jax
import jax.numpy as jnp
from jax import lax
from jax.experimental import pallas as pl
from jax.experimental.pallas import tpu as pltpu
from jax.sharding import PartitionSpec as P

STEPS = 4
ITERS = 2
LANES = 128
SUB = 8
F32 = jnp.float32
BF16 = jnp.bfloat16
HIGH = lax.Precision.HIGHEST
MESH = pl.DeviceIdType.MESH
NT = (((1,), (1,)), ((), ()))
TN = (((0,), (0,)), ((), ()))


def vmem():
    return pl.BlockSpec(memory_space=pltpu.VMEM)


def nt(a, b):
    return lax.dot_general(a, b, NT, precision=HIGH, preferred_element_type=F32)


def nn(a, b):
    return jnp.dot(a, b, precision=HIGH, preferred_element_type=F32)


def two_parts(x):
    hi = x.astype(BF16)
    lo = (x - hi.astype(F32)).astype(BF16)
    return jnp.concatenate([hi, lo], axis=0)


def orthonormal(inner, image, c_ref, y_ref):
    order, wide = image.shape
    blocks = order // SUB
    c_ref[:, 0:order] = inner
    c_ref[:, order:] = jnp.zeros((order, wide - order), F32)
    y_ref[...] = image
    row = lax.broadcasted_iota(jnp.int32, (SUB, wide), 0)

    @pl.loop(0, blocks)
    def panel(_):
        cs = [c_ref[q * SUB:(q + 1) * SUB, :] for q in range(blocks)]
        ys = [y_ref[q * SUB:(q + 1) * SUB, :] for q in range(blocks)]
        cols = [[jnp.broadcast_to(c[:, k:k + 1], (SUB, wide)) for c in cs] for k in range(SUB)]
        pivots = jnp.ones((SUB, wide), F32)
        for j in range(SUB):
            pivot = cols[j][0][j:j + 1]
            pivots = jnp.where(row == j, pivot, pivots)
            inverse = 1.0 / pivot
            y_row, c_row = ys[0][j:j + 1] * inverse, cs[0][j:j + 1] * inverse
            heads = [cols[k][0][j:j + 1] * inverse for k in range(SUB)]
            for q in range(blocks):
                factor = cols[j][q]
                if q == 0:
                    factor = jnp.where(row > j, factor, 0.0)
                ys[q] = ys[q] - factor * y_row
                cs[q] = cs[q] - factor * c_row
                for k in range(j + 1, SUB):
                    cols[k][q] = cols[k][q] - factor * heads[k]
        done = ys[0] * lax.rsqrt(pivots)
        cs = [pltpu.roll(c, wide - SUB, 1) for c in cs[1:]] + [jnp.zeros((SUB, wide), F32)]
        for q, (c, y) in enumerate(zip(cs, ys[1:] + [done])):
            c_ref[q * SUB:(q + 1) * SUB, :] = c
            y_ref[q * SUB:(q + 1) * SUB, :] = y


def basis_rows(gram_ref, q_ref, image_ref, c_ref, keep):
    image_ref[...] = gram_ref[:keep, :]

    @pl.loop(0, ITERS)
    def turn(_):
        image = image_ref[...]
        orthonormal(nt(image, image), image, c_ref, q_ref)
        image_ref[...] = nn(q_ref[...], gram_ref[...])

    return image_ref[...]


def gram_kernel(prior_ref, frames_ref, pp_ref, ps_ref, ss_ref):
    @pl.when(pl.program_id(0) == 0)
    def _():
        pp_ref[...] = jnp.zeros_like(pp_ref)
        ps_ref[...] = jnp.zeros_like(ps_ref)
        ss_ref[...] = jnp.zeros_like(ss_ref)

    prior, frames = prior_ref[...], frames_ref[...]
    pp_ref[...] += lax.dot_general(prior, prior, NT, preferred_element_type=F32)
    ps_ref[...] += jnp.dot(prior, frames, preferred_element_type=F32)
    ss_ref[...] += lax.dot_general(frames, frames, TN, preferred_element_type=F32)


def gram_of(prior, frames, tile):
    keep, rows = prior.shape
    wide = frames.shape[1]
    return pl.pallas_call(
        gram_kernel,
        grid=(rows // tile,),
        in_specs=[
            pl.BlockSpec((keep, tile), lambda i: (0, i)),
            pl.BlockSpec((tile, wide), lambda i: (i, 0)),
        ],
        out_specs=[
            pl.BlockSpec((keep, keep), lambda i: (0, 0)),
            pl.BlockSpec((keep, wide), lambda i: (0, 0)),
            pl.BlockSpec((wide, wide), lambda i: (0, 0)),
        ],
        out_shape=[
            jax.ShapeDtypeStruct((keep, keep), F32),
            jax.ShapeDtypeStruct((keep, wide), F32),
            jax.ShapeDtypeStruct((wide, wide), F32),
        ],
    )(prior, frames)


def meet(peers):
    barrier = pltpu.get_barrier_semaphore()
    for peer in peers:
        pl.semaphore_signal(barrier, inc=1, device_id=peer, device_id_type=MESH)
    pl.semaphore_wait(barrier, len(peers))


def sum_kernel(n, half, pp_ref, ps_ref, ss_ref, opp_ref, ops_ref, oss_ref, mine, got, full, s1, r1, s2, r2):
    me = lax.axis_index("rows")
    keep = pp_ref.shape[0]
    wide = ss_ref.shape[0]
    mine[...] = jnp.zeros_like(mine)
    mine[0:keep, 0:keep] = pp_ref[...]
    at = keep
    for c in range(wide // half):
        mine[at:at + keep, :] = ps_ref[:, c * half:(c + 1) * half]
        at += keep
    for a in range(wide // half):
        for b in range(a, wide // half):
            mine[at:at + half, :] = ss_ref[a * half:(a + 1) * half, b * half:(b + 1) * half]
            at += half
    peers = [{"rows": lax.rem(me + o, n)} for o in range(1, n)]
    meet(peers)
    piece = mine.shape[0] // n
    own = pl.ds(pl.multiple_of(me * piece, SUB), piece)
    first = []
    for o, peer in enumerate(peers):
        there = pl.ds(pl.multiple_of(peer["rows"] * piece, SUB), piece)
        copy = pltpu.make_async_remote_copy(
            src_ref=mine.at[there], dst_ref=got.at[o], send_sem=s1.at[o], recv_sem=r1.at[o],
            device_id=peer, device_id_type=MESH)
        copy.start()
        first.append(copy)
    total = mine[own, :]
    for o, copy in enumerate(first):
        copy.wait_recv()
        total = total + got[o]
    full[own, :] = total
    second = []
    for o, peer in enumerate(peers):
        copy = pltpu.make_async_remote_copy(
            src_ref=full.at[own], dst_ref=full.at[own], send_sem=s2.at[o], recv_sem=r2.at[o],
            device_id=peer, device_id_type=MESH)
        copy.start()
        second.append(copy)
    for copy in second:
        copy.wait_recv()
    opp_ref[...] = full[0:keep, 0:keep]
    at = keep
    for c in range(wide // half):
        ops_ref[:, c * half:(c + 1) * half] = full[at:at + keep, :]
        at += keep
    for a in range(wide // half):
        for b in range(a, wide // half):
            block = full[at:at + half, :]
            oss_ref[a * half:(a + 1) * half, b * half:(b + 1) * half] = block
            if b > a:
                oss_ref[b * half:(b + 1) * half, a * half:(a + 1) * half] = block.T
            at += half
    for copy in first + second:
        copy.wait_send()


def sum_over_rows(pp, ps, ss):
    n = lax.axis_size("rows")
    keep, wide = ps.shape
    parts = wide // LANES
    rows = keep + parts * keep + parts * (parts + 1) // 2 * LANES
    rows = pl.cdiv(rows, SUB * n) * SUB * n
    dma = pltpu.SemaphoreType.DMA((n - 1,))
    return pl.pallas_call(
        functools.partial(sum_kernel, n, LANES),
        out_shape=[jax.ShapeDtypeStruct(x.shape, F32) for x in (pp, ps, ss)],
        in_specs=[vmem()] * 3,
        out_specs=[vmem()] * 3,
        scratch_shapes=[
            pltpu.VMEM((rows, LANES), F32),
            pltpu.VMEM((n - 1, rows // n, LANES), F32),
            pltpu.VMEM((rows, LANES), F32),
            dma, dma, dma, dma,
        ],
        compiler_params=pltpu.CompilerParams(collective_id=0, has_side_effects=True),
    )(pp, ps, ss)


def steps_kernel(pp_ref, ps_ref, ss_ref, wf_ref, wp_ref, own_ref, gram, q, held, square, weights, cross, heads, corners):
    keep, wide = ps_ref.shape
    fresh = wide // STEPS
    gram[0:keep, 0:keep] = pp_ref[...]
    for k in range(STEPS):
        heads[k] = ps_ref[:, k * fresh:(k + 1) * fresh]
        corners[k] = ss_ref[k * fresh:(k + 1) * fresh, k * fresh:(k + 1) * fresh]
    cross[...] = ps_ref[...]
    span = weights.shape[1]
    lane = lax.broadcasted_iota(jnp.int32, (fresh, span), 1)
    row = lax.broadcasted_iota(jnp.int32, (fresh, span), 0)
    weights[...] = jnp.where(lane == row + wide, 1.0, 0.0)

    def step(k, carry):
        head = heads[k]
        gram[0:keep, keep:] = head
        gram[keep:, 0:keep] = head.T
        gram[keep:, keep:] = corners[k]
        image = basis_rows(gram, q, held, square, keep)
        basis = q[...]
        gram[0:keep, 0:keep] = nt(image, basis)
        fresh_rows = ss_ref[pl.ds(pl.multiple_of(k * fresh, fresh), fresh), :]
        following = nn(basis, jnp.concatenate([cross[...], fresh_rows], axis=0))
        cross[...] = following
        for m in range(STEPS):
            heads[m] = following[:, m * fresh:(m + 1) * fresh]
        place = jnp.where(lane == row + k * fresh, 1.0, 0.0)
        weights[...] = nn(basis, jnp.concatenate([weights[...], place], axis=0))
        return carry

    lax.fori_loop(0, STEPS, step, 0)
    wf_ref[...] = two_parts(weights[:, 0:wide])
    wp_ref[...] = two_parts(weights[:, wide:wide + keep])
    own_ref[...] = jnp.zeros_like(own_ref)
    own_ref[:, 0:keep] = gram[0:keep, 0:keep]


def steps_of(pp, ps, ss):
    keep, wide = ps.shape
    fresh = wide // STEPS
    span = pl.cdiv(wide + keep, LANES) * LANES
    return pl.pallas_call(
        steps_kernel,
        out_shape=[
            jax.ShapeDtypeStruct((2 * keep, wide), BF16),
            jax.ShapeDtypeStruct((2 * keep, keep), BF16),
            jax.ShapeDtypeStruct((keep, LANES), F32),
        ],
        in_specs=[vmem()] * 3,
        out_specs=[vmem()] * 3,
        scratch_shapes=[
            pltpu.VMEM((keep + fresh, keep + fresh), F32),
            pltpu.VMEM((keep, keep + fresh), F32),
            pltpu.VMEM((keep, keep + fresh), F32),
            pltpu.VMEM((keep, keep + fresh), F32),
            pltpu.VMEM((keep, span), F32),
            pltpu.VMEM((keep, wide), F32),
            pltpu.VMEM((STEPS, keep, fresh), F32),
            pltpu.VMEM((STEPS, fresh, fresh), F32),
        ],
    )(pp, ps, ss)


def modes_kernel(prior_ref, frames_ref, wf_ref, wp_ref, out_ref):
    keep = out_ref.shape[0]
    both = jnp.dot(wp_ref[...], prior_ref[...], preferred_element_type=F32)
    both += lax.dot_general(wf_ref[...], frames_ref[...], NT, preferred_element_type=F32)
    out_ref[...] = (both[:keep] + both[keep:]).astype(BF16)


def modes_of(prior, frames, wf, wp, tile):
    keep, rows = prior.shape
    wide = frames.shape[1]
    return pl.pallas_call(
        modes_kernel,
        grid=(rows // tile,),
        in_specs=[
            pl.BlockSpec((keep, tile), lambda i: (0, i)),
            pl.BlockSpec((tile, wide), lambda i: (i, 0)),
            pl.BlockSpec(wf.shape, lambda i: (0, 0)),
            pl.BlockSpec(wp.shape, lambda i: (0, 0)),
        ],
        out_specs=pl.BlockSpec((keep, tile), lambda i: (0, i)),
        out_shape=jax.ShapeDtypeStruct((keep, rows), BF16),
    )(prior, frames, wf, wp)


def cross_kernel(own_ref, other_ref, out_ref):
    @pl.when(pl.program_id(0) == 0)
    def _():
        out_ref[...] = jnp.zeros_like(out_ref)

    out_ref[...] += lax.dot_general(own_ref[...], other_ref[...], NT, preferred_element_type=F32)


def cross_of(own, other, tile):
    keep, rows = own.shape
    return pl.pallas_call(
        cross_kernel,
        grid=(rows // tile,),
        in_specs=[pl.BlockSpec((keep, tile), lambda i: (0, i))] * 2,
        out_specs=pl.BlockSpec((keep, keep), lambda i: (0, 0)),
        out_shape=jax.ShapeDtypeStruct((keep, keep), F32),
    )(own, other)


def pair_kernel(n, cross_ref, own_ref, cross_out, other_out, mine, got, s1, r1, s2, r2):
    me, group = lax.axis_index("rows"), lax.axis_index("tm")
    keep = cross_ref.shape[0]
    half = keep // 2
    mine[:, 0:keep] = cross_ref[0:half, :]
    mine[:, keep:2 * keep] = cross_ref[half:keep, :]
    peers = [{"rows": lax.rem(me + o, n)} for o in range(1, n)]
    twin = {"tm": 1 - group}
    meet(peers + [twin])
    swap = pltpu.make_async_remote_copy(
        src_ref=own_ref, dst_ref=other_out, send_sem=s2, recv_sem=r2, device_id=twin, device_id_type=MESH)
    copies = []
    for o, peer in enumerate(peers):
        copy = pltpu.make_async_remote_copy(
            src_ref=mine, dst_ref=got.at[o], send_sem=s1.at[o], recv_sem=r1.at[o],
            device_id=peer, device_id_type=MESH)
        copy.start()
        copies.append(copy)
    swap.start()
    total = mine[...]
    for o, copy in enumerate(copies):
        copy.wait_recv()
        total = total + got[o]
    cross_out[0:half, :] = total[:, 0:keep]
    cross_out[half:keep, :] = total[:, keep:2 * keep]
    swap.wait_recv()
    for copy in copies + [swap]:
        copy.wait_send()


def pair_sums(cross, own):
    n = lax.axis_size("rows")
    keep = cross.shape[0]
    dma = pltpu.SemaphoreType.DMA((n - 1,))
    return pl.pallas_call(
        functools.partial(pair_kernel, n),
        out_shape=[jax.ShapeDtypeStruct(x.shape, F32) for x in (cross, own)],
        in_specs=[vmem()] * 2,
        out_specs=[vmem()] * 2,
        scratch_shapes=[
            pltpu.VMEM((keep // 2, 2 * keep), F32),
            pltpu.VMEM((n - 1, keep // 2, 2 * keep), F32),
            dma, dma, pltpu.SemaphoreType.DMA, pltpu.SemaphoreType.DMA,
        ],
        compiler_params=pltpu.CompilerParams(collective_id=1, has_side_effects=True),
    )(cross, own)


def merge_kernel(cross_ref, own_ref, other_ref, mine_ref, theirs_ref, gram, q, held, square):
    keep = cross_ref.shape[0]
    half = keep // 2
    lead = lax.axis_index("tm") == 0
    cross = cross_ref[...]
    turned = cross.T
    own, other = own_ref[:, 0:keep], other_ref[:, 0:keep]
    gram[0:keep, 0:keep] = jnp.where(lead, own, other)
    gram[keep:, keep:] = jnp.where(lead, other, own)
    gram[0:keep, keep:] = jnp.where(lead, cross, turned)
    gram[keep:, 0:keep] = jnp.where(lead, turned, cross)
    basis_rows(gram, q, held, square, keep)
    part = jnp.where(lead, q[0:half, :], q[half:keep, :])
    mine_ref[...] = two_parts(jnp.where(lead, part[:, 0:keep], part[:, keep:]))
    theirs_ref[...] = two_parts(jnp.where(lead, part[:, keep:], part[:, 0:keep]))


def merge_basis(cross, own, other):
    keep = cross.shape[0]
    return pl.pallas_call(
        merge_kernel,
        out_shape=[jax.ShapeDtypeStruct((keep, keep), BF16)] * 2,
        in_specs=[vmem()] * 3,
        out_specs=[vmem()] * 2,
        scratch_shapes=[pltpu.VMEM((2 * keep, 2 * keep), F32), pltpu.VMEM((keep, 2 * keep), F32)]
        + [pltpu.VMEM((keep, 2 * keep), F32)] * 2,
    )(cross, own, other)


def merged_kernel(own_ref, other_ref, mine_ref, theirs_ref, out_ref):
    half = out_ref.shape[0]
    both = jnp.dot(mine_ref[...], own_ref[...], preferred_element_type=F32)
    both += jnp.dot(theirs_ref[...], other_ref[...], preferred_element_type=F32)
    out_ref[...] = (both[:half] + both[half:]).astype(BF16)


def merged_of(own, other, mine, theirs, tile):
    keep, rows = own.shape
    half = keep // 2
    return pl.pallas_call(
        merged_kernel,
        grid=(rows // tile,),
        in_specs=[pl.BlockSpec((keep, tile), lambda i: (0, i))] * 2
        + [pl.BlockSpec(mine.shape, lambda i: (0, 0))] * 2,
        out_specs=pl.BlockSpec((half, tile), lambda i: (0, i)),
        out_shape=jax.ShapeDtypeStruct((half, rows), BF16),
    )(own, other, mine, theirs)


def shards(prior, snapshots):
    prior, frames = prior[0].T, snapshots[0]
    rows = frames.shape[0]
    tile = 2048 if rows % 2048 == 0 else rows
    wide_tile = 4096 if rows % 4096 == 0 else rows
    pp, ps, ss = sum_over_rows(*gram_of(prior, frames, tile))
    wf, wp, own_gram = steps_of(pp, ps, ss)
    own = modes_of(prior, frames, wf, wp, tile)
    other = lax.ppermute(own, "tm", [(0, 1), (1, 0)])
    cross, other_gram = pair_sums(cross_of(own, other, wide_tile), own_gram)
    mine, theirs = merge_basis(cross, own_gram, other_gram)
    return merged_of(own, other, mine, theirs, wide_tile).T


def solution(mesh):
    in_specs = (P("tm", ("job", "rows"), None), P("tm", ("job", "rows"), None))
    out_specs = P(("job", "rows"), "tm")
    return jax.shard_map(shards, mesh=mesh, in_specs=in_specs, out_specs=out_specs, check_vma=False)
```

time: 389 us -> 124 us (0.32)
  other arithmetic: 133 us -> 0 us
  Pallas kernels: 0 us -> 115 us
  matrix products: 108 us -> 0 us
  waiting for transfers between devices: 82.8 us -> 7.5 us
  blocking collectives: 35.5 us -> 0 us
  between operations: 14.4 us -> 0.02 us
  local copies, waits for them, and re-layouts: 10.7 us -> 0 us
    another operation x50 -> x0, other arithmetic: 121 us -> none  [the longest x30 65.3 us: basis_of(): lower = jnp.linalg.cholesky(inner)]
    pallas_call x0 -> x8, Pallas kernels: none -> 115 us  [the longest x1 24.2 us: steps_of(): pl.pallas_call(steps_kernel, out_shape=[jax.ShapeDtypeStruct((2 * keep, w...]
    dot_general x36 -> x0, matrix products: 105 us -> none  [the longest x2 42.7 us: project(): jnp.dot(joined, basis, precision=lax.Precision.HIGHEST, preferred_element...]
    psum x1 -> x0, waiting for transfers between devices: 75.3 us -> none  [shards(): lax.psum(jnp.dot(whole.T, whole, preferred_element_type=jnp.float32), 'ro...]
    psum x1 -> x0, blocking collectives: 35.5 us -> none  [shards(): lax.psum(inner_rows(joined, joined).astype(jnp.bfloat16), 'rows')]
    select_n x1 -> x0, other arithmetic: 12.1 us -> none  [shards(): first = jnp.where(index == 0, modes, other)]
    unnamed x1 -> x0, local copies, waits for them, and re-layouts: 8.48 us -> none
  transfers between devices with their start and end apart: 2 -> 1, of which waited for: 2 -> 1; matrix products, arithmetic and copies ran while one was open for 0% -> 0% of each run, Pallas kernels for 0% -> 0%
where the time goes in v1:
time: 124 us; the launch traced here: 122 us
  Pallas kernels  115 us (93%)
  waiting for transfers between devices  7.5 us (6%)
    pallas_call x1, Pallas kernels, steps_of(): pl.pallas_call(steps_kernel, out_shape=[jax.ShapeDtypeStruct((2 * keep, w...  24.2 us
    pallas_call x1, Pallas kernels, sum_over_rows(): pl.pallas_call(functools.partial(sum_kernel, n, LANES), out_shape=[jax.Sh...  20.8 us
    pallas_call x1, Pallas kernels, modes_of(): pl.pallas_call(modes_kernel, grid=(rows // tile,), in_specs=[pl.BlockSpec...  18.2 us
    pallas_call x1, Pallas kernels, gram_of(): pl.pallas_call(gram_kernel, grid=(rows // tile,), in_specs=[pl.BlockSpec(...  18.2 us
    pallas_call x1, Pallas kernels, pair_sums(): pl.pallas_call(functools.partial(pair_kernel, n), out_shape=[jax.ShapeDty...  11.1 us
    pallas_call x1, Pallas kernels, merged_of(): pl.pallas_call(merged_kernel, grid=(rows // tile,), in_specs=[pl.BlockSpe...  8.4 us
    ppermute x1, waiting for transfers between devices, shards(): other = lax.ppermute(own, 'tm', [(0, 1), (1, 0)])  7.5 us
    pallas_call x1, Pallas kernels, cross_of(): pl.pallas_call(cross_kernel, grid=(rows // tile,), in_specs=[pl.BlockSpec...  7.12 us
  transfers between devices with their start and end apart: 1, of which 1 were waited for; matrix products, arithmetic and copies ran while one was open for 0% of the time, Pallas kernels for 0%

profile of v1, /device:TPU:0, one launch (start us, length us, event | category | flops | bytes accessed | tf_op | source)
XLA Modules:
  0.0 122.3 jit_solution(931321612953679703)
XLA Ops:
  0.0 18.2 %shard_map.28 = (f32[64,64]{1,0:T(8,128)}, f32[64,256]{1,0:T(8,128)}, f32[256,256]{1,0:T(8,128)}) custom-call(bf16[64,32768]{1,0:T(8,128)(2,1)} %bitcast.7, bf16[32768,256]{1,0:T(8,128)(2,1)} %bitcast.5), custom_call_target="tpu_custom_call" | custom-call | tf_op jit(solution)/shard_map/pallas_call | solution.py:103
  18.2 20.8 %shard_map.29 = (f32[64,64]{1,0:T(8,128)}, f32[64,256]{1,0:T(8,128)}, f32[256,256]{1,0:T(8,128)}) custom-call(f32[64,64]{1,0:T(8,128)} %get-tuple-element.18.pp_ref, f32[64,256]{1,0:T(8,128)} %get-tuple-element.19.ps_ref, f32[256,256]{1,0:T(8,128)} %get-tuple-element.20.ss_ref), custom_call_target="tpu_custom_call" | custom-call | tf_op jit(solution)/shard_map/pallas_call | solution.py:193
  39.0 24.2 %shard_map.30 = (bf16[128,256]{1,0:T(8,128)(2,1)}, bf16[128,64]{1,0:T(8,128)(2,1)}, f32[64,128]{1,0:T(8,128)}) custom-call(f32[64,64]{1,0:T(8,128)} %get-tuple-element.21.pp_ref, f32[64,256]{1,0:T(8,128)} %get-tuple-element.22.ps_ref, f32[256,256]{1,0:T(8,128)} %get-tuple-element.23.ss_ref), custom_call_target="tpu_custom_call" | custom-call | tf_op jit(solution)/shard_map/pallas_call | solution.py:249
  63.3 18.2 %shard_map.31.own_ref = bf16[64,32768]{1,0:T(8,128)(2,1)} custom-call(bf16[64,32768]{1,0:T(8,128)(2,1)} %bitcast.8, bf16[32768,256]{1,0:T(8,128)(2,1)} %bitcast.6, bf16[128,256]{1,0:T(8,128)(2,1)} %get-tuple-element.24.wf_ref, bf16[128,64]{1,0:T(8,128)(2,1)} %get-tuple-element.25.wp_ref), custom_call_target="tpu_custom_call" | custom-call | tf_op jit(solution)/shard_map/pallas_call | solution.py:281
  81.5 0.0 collective-permute-start
  81.5 7.5 %collective-permute-done.other_ref = bf16[64,32768]{1,0:T(8,128)(2,1)} collective-permute-done((bf16[64,32768]{1,0:T(8,128)(2,1)}, bf16[64,32768]{1,0:T(8,128)(2,1)}, u32[]{:S(2)}, u32[]{:S(2)}) %collective-permute-start) | collective-permute-done | bytes 4194336 | tf_op jit(solution)/shard_map/ppermute | solution.py:419
  89.0 7.1 %shard_map.32.cross_ref = f32[64,64]{1,0:T(8,128)} custom-call(bf16[64,32768]{1,0:T(8,128)(2,1)} %shard_map.31.own_ref, bf16[64,32768]{1,0:T(8,128)(2,1)} %collective-permute-done.other_ref), custom_call_target="tpu_custom_call" | custom-call | tf_op jit(solution)/shard_map/pallas_call | solution.py:305
  96.1 11.1 %shard_map.33 = (f32[64,64]{1,0:T(8,128)}, f32[64,128]{1,0:T(8,128)}) custom-call(f32[64,64]{1,0:T(8,128)} %shard_map.32.cross_ref, f32[64,128]{1,0:T(8,128)} %get-tuple-element.26.own_ref), custom_call_target="tpu_custom_call" | custom-call | tf_op jit(solution)/shard_map/pallas_call | solution.py:348
  107.2 6.7 %shard_map.34 = (bf16[64,64]{1,0:T(8,128)(2,1)}, bf16[64,64]{1,0:T(8,128)(2,1)}) custom-call(f32[64,64]{1,0:T(8,128)} %get-tuple-element.27.cross_ref, f32[64,128]{1,0:T(8,128)} %get-tuple-element.26.own_ref, f32[64,128]{1,0:T(8,128)} %get-tuple-element.28.other_ref), custom_call_target="tpu_custom_call" | custom-call | tf_op jit(solution)/shard_map/pallas_call | solution.py:381
  113.9 8.4 %shard_map.35 = bf16[32,32768]{1,0:T(8,128)(2,1)} custom-call(bf16[64,32768]{1,0:T(8,128)(2,1)} %shard_map.31.own_ref, bf16[64,32768]{1,0:T(8,128)(2,1)} %collective-permute-done.other_ref, bf16[64,64]{1,0:T(8,128)(2,1)} %get-tuple-element.29.mine_ref, bf16[64,64]{1,0:T(8,128)(2,1)} %get-tuple-element.30.theirs_ref), custom_call_target="tpu_custom_call" | custom-call | tf_op jit(solution)/shard_map/pallas_call | solution.py:401
Async XLA Ops:
  81.5 7.5 %collective-permute-start = (bf16[64,32768]{1,0:T(8,128)(2,1)}, bf16[64,32768]{1,0:T(8,128)(2,1)}, u32[]{:S(2)}, u32[]{:S(2)}) collective-permute-start(bf16[64,32768]{1,0:T(8,128)(2,1)} %shard_map.31.own_ref), channel_id=1, source_target_pairs={{0,8},{8,0},{1,9},{9,1},{2,10},{10,2},{3,11},{11,3},{4,12},{12,4},... | collective-permute-start | bytes 12582920 | tf_op jit(solution)/shard_map/ppermute | solution.py:419

commit v2 on v1

--- a/solution.py
+++ b/solution.py
@@ -411,8 +411,8 @@
 def shards(prior, snapshots):
     prior, frames = prior[0].T, snapshots[0]
     rows = frames.shape[0]
-    tile = 2048 if rows % 2048 == 0 else rows
-    wide_tile = 4096 if rows % 4096 == 0 else rows
+    tile = 4096 if rows % 4096 == 0 else rows
+    wide_tile = 8192 if rows % 8192 == 0 else rows
     pp, ps, ss = sum_over_rows(*gram_of(prior, frames, tile))
     wf, wp, own_gram = steps_of(pp, ps, ss)
     own = modes_of(prior, frames, wf, wp, tile)

time: 124 us -> 112 us (0.903)
  Pallas kernels: 115 us -> 103 us
    pallas_call x1, Pallas kernels: 18.2 us -> 14.3 us  [gram_of(): pl.pallas_call(gram_kernel, grid=(rows // tile,), in_specs=[pl.BlockSpec(...]
    pallas_call x1, Pallas kernels: 18.2 us -> 14.4 us  [modes_of(): pl.pallas_call(modes_kernel, grid=(rows // tile,), in_specs=[pl.BlockSpec...]
    pallas_call x1, Pallas kernels: 8.4 us -> 6.48 us  [merged_of(): pl.pallas_call(merged_kernel, grid=(rows // tile,), in_specs=[pl.BlockSpe...]
    pallas_call x1, Pallas kernels: 7.12 us -> 5.33 us  [cross_of(): pl.pallas_call(cross_kernel, grid=(rows // tile,), in_specs=[pl.BlockSpec...]
where the time goes in v2:
time: 112 us; the launch traced here: 111 us
  Pallas kernels  103 us (92%)
  waiting for transfers between devices  7.5 us (7%)
    pallas_call x1, Pallas kernels, steps_of(): pl.pallas_call(steps_kernel, out_shape=[jax.ShapeDtypeStruct((2 * keep, w...  24.2 us
    pallas_call x1, Pallas kernels, sum_over_rows(): pl.pallas_call(functools.partial(sum_kernel, n, LANES), out_shape=[jax.Sh...  20.8 us
    pallas_call x1, Pallas kernels, modes_of(): pl.pallas_call(modes_kernel, grid=(rows // tile,), in_specs=[pl.BlockSpec...  14.4 us
    pallas_call x1, Pallas kernels, gram_of(): pl.pallas_call(gram_kernel, grid=(rows // tile,), in_specs=[pl.BlockSpec(...  14.3 us
    pallas_call x1, Pallas kernels, pair_sums(): pl.pallas_call(functools.partial(pair_kernel, n), out_shape=[jax.ShapeDty...  11 us
    ppermute x1, waiting for transfers between devices, shards(): other = lax.ppermute(own, 'tm', [(0, 1), (1, 0)])  7.5 us
    pallas_call x1, Pallas kernels, merge_basis(): pl.pallas_call(merge_kernel, out_shape=[jax.ShapeDtypeStruct((keep, keep)...  6.74 us
    pallas_call x1, Pallas kernels, merged_of(): pl.pallas_call(merged_kernel, grid=(rows // tile,), in_specs=[pl.BlockSpe...  6.48 us
  transfers between devices with their start and end apart: 1, of which 1 were waited for; matrix products, arithmetic and copies ran while one was open for 0% of the time, Pallas kernels for 0%

profile of v2, /device:TPU:0, one launch (start us, length us, event | category | flops | bytes accessed | tf_op | source)
XLA Modules:
  0.0 110.8 jit_solution(1472036310166107803)
XLA Ops:
  0.0 14.3 %shard_map.28 = (f32[64,64]{1,0:T(8,128)}, f32[64,256]{1,0:T(8,128)}, f32[256,256]{1,0:T(8,128)}) custom-call(bf16[64,32768]{1,0:T(8,128)(2,1)} %bitcast.7, bf16[32768,256]{1,0:T(8,128)(2,1)} %bitcast.5), custom_call_target="tpu_custom_call" | custom-call | tf_op jit(solution)/shard_map/pallas_call | solution.py:103
  14.3 20.8 %shard_map.29 = (f32[64,64]{1,0:T(8,128)}, f32[64,256]{1,0:T(8,128)}, f32[256,256]{1,0:T(8,128)}) custom-call(f32[64,64]{1,0:T(8,128)} %get-tuple-element.18.pp_ref, f32[64,256]{1,0:T(8,128)} %get-tuple-element.19.ps_ref, f32[256,256]{1,0:T(8,128)} %get-tuple-element.20.ss_ref), custom_call_target="tpu_custom_call" | custom-call | tf_op jit(solution)/shard_map/pallas_call | solution.py:193
  35.1 24.2 %shard_map.30 = (bf16[128,256]{1,0:T(8,128)(2,1)}, bf16[128,64]{1,0:T(8,128)(2,1)}, f32[64,128]{1,0:T(8,128)}) custom-call(f32[64,64]{1,0:T(8,128)} %get-tuple-element.21.pp_ref, f32[64,256]{1,0:T(8,128)} %get-tuple-element.22.ps_ref, f32[256,256]{1,0:T(8,128)} %get-tuple-element.23.ss_ref), custom_call_target="tpu_custom_call" | custom-call | tf_op jit(solution)/shard_map/pallas_call | solution.py:249
  59.3 14.4 %shard_map.31.own_ref = bf16[64,32768]{1,0:T(8,128)(2,1)} custom-call(bf16[64,32768]{1,0:T(8,128)(2,1)} %bitcast.8, bf16[32768,256]{1,0:T(8,128)(2,1)} %bitcast.6, bf16[128,256]{1,0:T(8,128)(2,1)} %get-tuple-element.24.wf_ref, bf16[128,64]{1,0:T(8,128)(2,1)} %get-tuple-element.25.wp_ref), custom_call_target="tpu_custom_call" | custom-call | tf_op jit(solution)/shard_map/pallas_call | solution.py:281
  73.7 0.0 collective-permute-start
  73.7 7.5 %collective-permute-done.other_ref = bf16[64,32768]{1,0:T(8,128)(2,1)} collective-permute-done((bf16[64,32768]{1,0:T(8,128)(2,1)}, bf16[64,32768]{1,0:T(8,128)(2,1)}, u32[]{:S(2)}, u32[]{:S(2)}) %collective-permute-start) | collective-permute-done | bytes 4194336 | tf_op jit(solution)/shard_map/ppermute | solution.py:419
  81.2 5.3 %shard_map.32.cross_ref = f32[64,64]{1,0:T(8,128)} custom-call(bf16[64,32768]{1,0:T(8,128)(2,1)} %shard_map.31.own_ref, bf16[64,32768]{1,0:T(8,128)(2,1)} %collective-permute-done.other_ref), custom_call_target="tpu_custom_call" | custom-call | tf_op jit(solution)/shard_map/pallas_call | solution.py:305
  86.5 11.0 %shard_map.33 = (f32[64,64]{1,0:T(8,128)}, f32[64,128]{1,0:T(8,128)}) custom-call(f32[64,64]{1,0:T(8,128)} %shard_map.32.cross_ref, f32[64,128]{1,0:T(8,128)} %get-tuple-element.26.own_ref), custom_call_target="tpu_custom_call" | custom-call | tf_op jit(solution)/shard_map/pallas_call | solution.py:348
  97.6 6.7 %shard_map.34 = (bf16[64,64]{1,0:T(8,128)(2,1)}, bf16[64,64]{1,0:T(8,128)(2,1)}) custom-call(f32[64,64]{1,0:T(8,128)} %get-tuple-element.27.cross_ref, f32[64,128]{1,0:T(8,128)} %get-tuple-element.26.own_ref, f32[64,128]{1,0:T(8,128)} %get-tuple-element.28.other_ref), custom_call_target="tpu_custom_call" | custom-call | tf_op jit(solution)/shard_map/pallas_call | solution.py:381
  104.3 6.5 %shard_map.35 = bf16[32,32768]{1,0:T(8,128)(2,1)} custom-call(bf16[64,32768]{1,0:T(8,128)(2,1)} %shard_map.31.own_ref, bf16[64,32768]{1,0:T(8,128)(2,1)} %collective-permute-done.other_ref, bf16[64,64]{1,0:T(8,128)(2,1)} %get-tuple-element.29.mine_ref, bf16[64,64]{1,0:T(8,128)(2,1)} %get-tuple-element.30.theirs_ref), custom_call_target="tpu_custom_call" | custom-call | tf_op jit(solution)/shard_map/pallas_call | solution.py:401
Async XLA Ops:
  73.7 7.5 %collective-permute-start = (bf16[64,32768]{1,0:T(8,128)(2,1)}, bf16[64,32768]{1,0:T(8,128)(2,1)}, u32[]{:S(2)}, u32[]{:S(2)}) collective-permute-start(bf16[64,32768]{1,0:T(8,128)(2,1)} %shard_map.31.own_ref), channel_id=1, source_target_pairs={{0,8},{8,0},{1,9},{9,1},{2,10},{10,2},{3,11},{11,3},{4,12},{12,4},... | collective-permute-start | bytes 12582920 | tf_op jit(solution)/shard_map/ppermute | solution.py:419

commit v3 on v2

--- a/solution.py
+++ b/solution.py
@@ -411,8 +411,8 @@
 def shards(prior, snapshots):
     prior, frames = prior[0].T, snapshots[0]
     rows = frames.shape[0]
-    tile = 4096 if rows % 4096 == 0 else rows
-    wide_tile = 8192 if rows % 8192 == 0 else rows
+    tile = 8192 if rows % 8192 == 0 else rows
+    wide_tile = 16384 if rows % 16384 == 0 else rows
     pp, ps, ss = sum_over_rows(*gram_of(prior, frames, tile))
     wf, wp, own_gram = steps_of(pp, ps, ss)
     own = modes_of(prior, frames, wf, wp, tile)

time: 112 us -> 107 us (0.955)
  Pallas kernels: 103 us -> 98.8 us
    pallas_call x1, Pallas kernels: 14.4 us -> 12.6 us  [modes_of(): pl.pallas_call(modes_kernel, grid=(rows // tile,), in_specs=[pl.BlockSpec...]
    pallas_call x1, Pallas kernels: 14.3 us -> 12.6 us  [gram_of(): pl.pallas_call(gram_kernel, grid=(rows // tile,), in_specs=[pl.BlockSpec(...]
where the time goes in v3:
time: 107 us; the launch traced here: 106 us
  Pallas kernels  98.8 us (92%)
  waiting for transfers between devices  7.5 us (7%)
    pallas_call x1, Pallas kernels, steps_of(): pl.pallas_call(steps_kernel, out_shape=[jax.ShapeDtypeStruct((2 * keep, w...  24.2 us
    pallas_call x1, Pallas kernels, sum_over_rows(): pl.pallas_call(functools.partial(sum_kernel, n, LANES), out_shape=[jax.Sh...  20.8 us
    pallas_call x1, Pallas kernels, gram_of(): pl.pallas_call(gram_kernel, grid=(rows // tile,), in_specs=[pl.BlockSpec(...  12.6 us
    pallas_call x1, Pallas kernels, modes_of(): pl.pallas_call(modes_kernel, grid=(rows // tile,), in_specs=[pl.BlockSpec...  12.6 us
    pallas_call x1, Pallas kernels, pair_sums(): pl.pallas_call(functools.partial(pair_kernel, n), out_shape=[jax.ShapeDty...  11.1 us
    ppermute x1, waiting for transfers between devices, shards(): other = lax.ppermute(own, 'tm', [(0, 1), (1, 0)])  7.5 us
    pallas_call x1, Pallas kernels, merge_basis(): pl.pallas_call(merge_kernel, out_shape=[jax.ShapeDtypeStruct((keep, keep)...  6.74 us
    pallas_call x1, Pallas kernels, merged_of(): pl.pallas_call(merged_kernel, grid=(rows // tile,), in_specs=[pl.BlockSpe...  5.9 us
  transfers between devices with their start and end apart: 1, of which 1 were waited for; matrix products, arithmetic and copies ran while one was open for 0% of the time, Pallas kernels for 0%

profile of v3, /device:TPU:0, one launch (start us, length us, event | category | flops | bytes accessed | tf_op | source)
XLA Modules:
  0.0 106.3 jit_solution(4042607995504539091)
XLA Ops:
  0.0 12.6 %shard_map.28 = (f32[64,64]{1,0:T(8,128)}, f32[64,256]{1,0:T(8,128)}, f32[256,256]{1,0:T(8,128)}) custom-call(bf16[64,32768]{1,0:T(8,128)(2,1)} %bitcast.7, bf16[32768,256]{1,0:T(8,128)(2,1)} %bitcast.5), custom_call_target="tpu_custom_call" | custom-call | tf_op jit(solution)/shard_map/pallas_call | solution.py:103
  12.6 20.8 %shard_map.29 = (f32[64,64]{1,0:T(8,128)}, f32[64,256]{1,0:T(8,128)}, f32[256,256]{1,0:T(8,128)}) custom-call(f32[64,64]{1,0:T(8,128)} %get-tuple-element.18.pp_ref, f32[64,256]{1,0:T(8,128)} %get-tuple-element.19.ps_ref, f32[256,256]{1,0:T(8,128)} %get-tuple-element.20.ss_ref), custom_call_target="tpu_custom_call" | custom-call | tf_op jit(solution)/shard_map/pallas_call | solution.py:193
  33.5 24.2 %shard_map.30 = (bf16[128,256]{1,0:T(8,128)(2,1)}, bf16[128,64]{1,0:T(8,128)(2,1)}, f32[64,128]{1,0:T(8,128)}) custom-call(f32[64,64]{1,0:T(8,128)} %get-tuple-element.21.pp_ref, f32[64,256]{1,0:T(8,128)} %get-tuple-element.22.ps_ref, f32[256,256]{1,0:T(8,128)} %get-tuple-element.23.ss_ref), custom_call_target="tpu_custom_call" | custom-call | tf_op jit(solution)/shard_map/pallas_call | solution.py:249
  57.7 12.6 %shard_map.31.own_ref = bf16[64,32768]{1,0:T(8,128)(2,1)} custom-call(bf16[64,32768]{1,0:T(8,128)(2,1)} %bitcast.8, bf16[32768,256]{1,0:T(8,128)(2,1)} %bitcast.6, bf16[128,256]{1,0:T(8,128)(2,1)} %get-tuple-element.24.wf_ref, bf16[128,64]{1,0:T(8,128)(2,1)} %get-tuple-element.25.wp_ref), custom_call_target="tpu_custom_call" | custom-call | tf_op jit(solution)/shard_map/pallas_call | solution.py:281
  70.3 0.0 collective-permute-start
  70.3 7.5 %collective-permute-done.other_ref = bf16[64,32768]{1,0:T(8,128)(2,1)} collective-permute-done((bf16[64,32768]{1,0:T(8,128)(2,1)}, bf16[64,32768]{1,0:T(8,128)(2,1)}, u32[]{:S(2)}, u32[]{:S(2)}) %collective-permute-start) | collective-permute-done | bytes 4194336 | tf_op jit(solution)/shard_map/ppermute | solution.py:419
  77.8 4.8 %shard_map.32.cross_ref = f32[64,64]{1,0:T(8,128)} custom-call(bf16[64,32768]{1,0:T(8,128)(2,1)} %shard_map.31.own_ref, bf16[64,32768]{1,0:T(8,128)(2,1)} %collective-permute-done.other_ref), custom_call_target="tpu_custom_call" | custom-call | tf_op jit(solution)/shard_map/pallas_call | solution.py:305
  82.6 11.1 %shard_map.33 = (f32[64,64]{1,0:T(8,128)}, f32[64,128]{1,0:T(8,128)}) custom-call(f32[64,64]{1,0:T(8,128)} %shard_map.32.cross_ref, f32[64,128]{1,0:T(8,128)} %get-tuple-element.26.own_ref), custom_call_target="tpu_custom_call" | custom-call | tf_op jit(solution)/shard_map/pallas_call | solution.py:348
  93.7 6.7 %shard_map.34 = (bf16[64,64]{1,0:T(8,128)(2,1)}, bf16[64,64]{1,0:T(8,128)(2,1)}) custom-call(f32[64,64]{1,0:T(8,128)} %get-tuple-element.27.cross_ref, f32[64,128]{1,0:T(8,128)} %get-tuple-element.26.own_ref, f32[64,128]{1,0:T(8,128)} %get-tuple-element.28.other_ref), custom_call_target="tpu_custom_call" | custom-call | tf_op jit(solution)/shard_map/pallas_call | solution.py:381
  100.4 5.9 %shard_map.35 = bf16[32,32768]{1,0:T(8,128)(2,1)} custom-call(bf16[64,32768]{1,0:T(8,128)(2,1)} %shard_map.31.own_ref, bf16[64,32768]{1,0:T(8,128)(2,1)} %collective-permute-done.other_ref, bf16[64,64]{1,0:T(8,128)(2,1)} %get-tuple-element.29.mine_ref, bf16[64,64]{1,0:T(8,128)(2,1)} %get-tuple-element.30.theirs_ref), custom_call_target="tpu_custom_call" | custom-call | tf_op jit(solution)/shard_map/pallas_call | solution.py:401
Async XLA Ops:
  70.3 7.5 %collective-permute-start = (bf16[64,32768]{1,0:T(8,128)(2,1)}, bf16[64,32768]{1,0:T(8,128)(2,1)}, u32[]{:S(2)}, u32[]{:S(2)}) collective-permute-start(bf16[64,32768]{1,0:T(8,128)(2,1)} %shard_map.31.own_ref), channel_id=1, source_target_pairs={{0,8},{8,0},{1,9},{9,1},{2,10},{10,2},{3,11},{11,3},{4,12},{12,4},... | collective-permute-start | bytes 12582920 | tf_op jit(solution)/shard_map/ppermute | solution.py:419
